TPU v7x, 256 devices: a whole 4x4x8 slice. The times are simulated.
256 devices in a mesh: seq: 32 (over y, z), head: 8 (over x, core).
Axes of the slice: x: 4, y: 4, z: 8, core: 2. Of those that a mesh axis runs over, the one named last changes fastest.
Arguments:
- queries: bfloat16 [16384, 8192], P('seq', 'head'), may hold values from -4 to 4
- key_vecs: bfloat16 [16384, 8192], P('seq', 'head'), may hold values from -4 to 4
- value_vecs: bfloat16 [16384, 8192], P('seq', 'head'), may hold values from -6 to 6
- log_decay: float32 [16384, 64], P('seq', 'head'), may hold values from -3 to 0, as said below
- norm_gain: float32 [8192], P('head'), may hold values from 0.1 to 1.9
- cotangent: bfloat16 [16384, 8192], P('seq', 'head'), may hold values from -6 to 6
Outputs:
- attended: bfloat16 [16384, 8192], P('seq', 'head')
- grad_queries: bfloat16 [16384, 8192], P('seq', 'head')
- grad_keys: bfloat16 [16384, 8192], P('seq', 'head')
- grad_values: bfloat16 [16384, 8192], P('seq', 'head')
Inputs may be any that keep to these rules, and one draw needn't show every extreme that they name: `log_decay`: every entry is negative.
All inputs are finite; a program needn't handle non-finite values.
Results may differ from a plain program's by a relative error of at most 0.0051.
Values sent between devices are 32-bit elements; how exact they have to be, the bound alone decides.
A program may use at most 128 MiB of HBM per device.

v0:
```python
import jax
import jax.numpy as jnp
from jax import lax
from jax.sharding import PartitionSpec as P

HEAD_TOTAL = 64
HEAD_DIM = 128
BLOCK = 512


highest = lax.Precision.HIGHEST
epsilon = 1e-06


def prefix(part, axis, combine, identity, reverse):
    count = lax.axis_size(axis)
    place = lax.axis_index(axis)
    ahead = count - 1 - place if reverse else place
    gathered = jax.tree.map(lambda a: lax.all_gather(a, axis), part)
    state = jax.tree.map(lambda a, e: jnp.zeros_like(a) + jnp.asarray(e, a.dtype), part, identity)

    def one(turn, state):
        source = count - 1 - turn if reverse else turn
        return combine(
            state, jax.tree.map(lambda a: lax.dynamic_index_in_dim(a, source, 0, False), gathered)
        )

    return lax.fori_loop(0, ahead, one, state)


def block_decay(cumulative):
    transposed = cumulative.T
    spread_log = transposed[:, :, None] - transposed[:, None, :]
    length = cumulative.shape[0]
    causal = (jnp.arange(length)[:, None] >= jnp.arange(length)[None, :])[None]
    return jnp.where(causal, jnp.exp(jnp.where(causal, spread_log, 0.0)), 0.0)


def chain_combine(earlier, later):
    return (earlier[0] + later[0], jnp.exp(later[0])[:, None, None] * earlier[1] + later[1])


def on_device(queries, key_vecs, value_vecs, log_decay, norm_gain, cotangent):
    tokens = queries.shape[0]
    head_count = queries.shape[1] // HEAD_DIM
    block_count = tokens // BLOCK
    feature_count = HEAD_TOTAL * HEAD_DIM
    state_shape = (head_count, HEAD_DIM, HEAD_DIM)

    def to_blocks(array):
        return array.reshape(block_count, BLOCK, head_count, HEAD_DIM)

    query_blocks = to_blocks(queries)
    key_blocks = to_blocks(key_vecs)
    value_blocks = to_blocks(value_vecs)
    cumulative = jnp.cumsum(log_decay.reshape(block_count, BLOCK, head_count), axis=1)
    totals = cumulative[:, -1, :]
    device_total = jnp.sum(totals, axis=0)
    prior_sum = jnp.cumsum(totals, axis=0) - totals
    later_sum = device_total[None] - jnp.cumsum(totals, axis=0)
    lead_scale = jnp.exp(cumulative)[..., None]
    trail_scale = jnp.exp(totals[:, None, :] - cumulative)[..., None]
    zero_state = jnp.zeros(state_shape, jnp.float32)
    zero_total = jnp.zeros((head_count,), jnp.float32)
    query_float = query_blocks.astype(jnp.float32)
    pieces = jnp.einsum(
        "bshd,bshe->bhde",
        key_blocks.astype(jnp.float32) * trail_scale,
        value_blocks.astype(jnp.float32),
        precision=highest,
    )

    def advance(running, scan_item):
        state_piece, block_total = scan_item
        return (jnp.exp(block_total)[:, None, None] * running + state_piece, running)

    local_end, local_before = lax.scan(advance, zero_state, (pieces, totals))

    def forward_inner(inputs):
        query_block, key_block, value_block, block_cumul = inputs
        decays = block_decay(block_cumul)
        scores = jnp.einsum(
            "thd,shd->hts", query_block, key_block, preferred_element_type=jnp.float32
        )
        weights = (scores * decays).astype(jnp.bfloat16)
        return jnp.einsum("hts,shd->thd", weights, value_block, preferred_element_type=jnp.float32)

    inner_out = lax.map(forward_inner, (query_blocks, key_blocks, value_blocks, cumulative))
    prefix_pair = prefix(
        (device_total, local_end), "seq", chain_combine, (zero_total, zero_state), False
    )
    incoming = prefix_pair[1]
    states_before = local_before + jnp.exp(prior_sum)[:, :, None, None] * incoming[None]
    outer_out = lead_scale * jnp.einsum(
        "bthd,bhde->bthe", query_float, states_before, precision=highest
    )
    flat_out = (inner_out + outer_out).reshape(tokens, head_count * HEAD_DIM)
    scaled_grad = cotangent.astype(jnp.float32) * norm_gain[None]
    square_sum, inner_sum = lax.psum(
        (jnp.sum(flat_out * flat_out, axis=1), jnp.sum(scaled_grad * flat_out, axis=1)), "head"
    )
    inverse = lax.rsqrt(square_sum / feature_count + epsilon)
    normed = flat_out * inverse[:, None]
    attended = (normed * norm_gain[None]).astype(jnp.bfloat16)
    mean_term = inverse * inner_sum / feature_count
    grad_out = (inverse[:, None] * (scaled_grad - normed * mean_term[:, None])).astype(jnp.bfloat16)
    grad_blocks = to_blocks(grad_out)
    grad_float = grad_blocks.astype(jnp.float32)
    grad_pieces = jnp.einsum(
        "bthd,bthe->bhde", query_float * lead_scale, grad_float, precision=highest
    )

    def retreat(running, scan_item):
        grad_piece, block_total = scan_item
        return (grad_piece + jnp.exp(block_total)[:, None, None] * running, running)

    local_start, local_after = lax.scan(retreat, zero_state, (grad_pieces, totals), reverse=True)

    def backward_inner(inputs):
        query_block, key_block, value_block, block_cumul, grad_block = inputs
        decays = block_decay(block_cumul)
        scores = jnp.einsum(
            "thd,shd->hts", query_block, key_block, preferred_element_type=jnp.float32
        )
        weights = (scores * decays).astype(jnp.bfloat16)
        grad_scores = jnp.einsum(
            "thd,shd->hts", grad_block, value_block, preferred_element_type=jnp.float32
        )
        grad_weights = (grad_scores * decays).astype(jnp.bfloat16)
        inner_query = jnp.einsum(
            "hts,shd->thd", grad_weights, key_block, preferred_element_type=jnp.float32
        )
        inner_key = jnp.einsum(
            "hts,thd->shd", grad_weights, query_block, preferred_element_type=jnp.float32
        )
        inner_value = jnp.einsum(
            "hts,thd->shd", weights, grad_block, preferred_element_type=jnp.float32
        )
        return (inner_query, inner_key, inner_value)

    inner_query, inner_key, inner_value = lax.map(
        backward_inner, (query_blocks, key_blocks, value_blocks, cumulative, grad_blocks)
    )
    suffix_pair = prefix(
        (device_total, local_start), "seq", chain_combine, (zero_total, zero_state), True
    )
    outgoing = suffix_pair[1]
    after_grad = local_after + jnp.exp(later_sum)[:, :, None, None] * outgoing[None]
    grad_queries = inner_query + lead_scale * jnp.einsum(
        "bthe,bhde->bthd", grad_float, states_before, precision=highest
    )
    grad_keys = inner_key + trail_scale * jnp.einsum(
        "bshe,bhde->bshd", value_blocks.astype(jnp.float32), after_grad, precision=highest
    )
    grad_values = inner_value + trail_scale * jnp.einsum(
        "bshd,bhde->bshe", key_blocks.astype(jnp.float32), after_grad, precision=highest
    )
    flat_shape = (tokens, head_count * HEAD_DIM)
    return (
        attended,
        grad_queries.reshape(flat_shape).astype(jnp.bfloat16),
        grad_keys.reshape(flat_shape).astype(jnp.bfloat16),
        grad_values.reshape(flat_shape).astype(jnp.bfloat16),
    )


def solution(mesh):
    return jax.shard_map(
        on_device,
        mesh=mesh,
        in_specs=(
            P("seq", "head"),
            P("seq", "head"),
            P("seq", "head"),
            P("seq", "head"),
            P("head"),
            P("seq", "head"),
        ),
        out_specs=(P("seq", "head"), P("seq", "head"), P("seq", "head"), P("seq", "head")),
        check_vma=False,
    )
```

profile of v0, /device:TPU:1, one launch (start us, length us, event | category | flops | bytes accessed | tf_op | source)
XLA Modules:
  0.0 414.5 jit_solution(7851424497753805606)
XLA Ops:
  7.2 2.3 reduce-window.6
  12.3 2.1 fusion.13
  14.5 1.5 copy.119
  16.0 37.4 %all-gather = f32[32,1,8]{2,1,0:T(1,128)S(1)} all-gather(f32[1,1,8]{2,1,0:T(1,128)S(1)} %copy.91), channel_id=2, replica_groups=mesh['seq'=32,'head'=8] {'seq'}, dimensions={0}, use_global_device_ids=true | all-gather | bytes 1056 | tf_op jit(solution)/shard_map/all_gather | solution.py:19
  53.6 4.2 %multiply_convert_fusion.1 = bf16[8,512,512]{2,1,0:T(8,128)(2,1)S(1)} fusion(f32[8,512]{1,0:T(8,128)S(1)} %fusion.42, pred[512,512]{1,0:T(8,128)(4,1)S(1)} %iota_compare_fusion, bf16[512,8,128]{0,2,1:T(8,128)(2,1)S(1)} %bitcast.161, bf16[512,1024]{1,0:T(8,128)(2,1)} %param.11), kind=kOutput, calls=%fused_computation.5 | convolution fusion | flops 547356672 | bytes 6569984 | tf_op jit(solution)/shard_map/while/body/eval_jaxpr/thd,shd->hts/dot_general | solution.py:82
  57.8 1.9 copy-done.1
  59.8 2.8 fusion.19
  62.6 94.8 %all-gather.6.cloned.1.call-done = f32[256,128,128]{2,1,0:T(8,128)} async-done(((f32[8,128,128]{2,1,0:T(8,128)}), f32[256,128,128]{2,1,0:T(8,128)}) %all-gather.6.cloned.1.call-update) | async-done | bytes 16777232 | tf_op jit(solution)/shard_map/all_gather | solution.py:19
  157.5 4.3 %multiply_reduce_fusion.1 = (f32[512]{0:T(512)S(1)}, f32[1,512,8,128]{1,3,2,0:T(8,128)}) fusion(bf16[512,8,128]{0,2,1:T(8,128)(2,1)S(1)} %bitcast.162, f32[8,128,128]{2,1,0:T(8,128)S(1)} %get-tuple-element.207, f32[8]{0:T(128)S(1)} %get-tuple-element.275, f32[512,8]{0,1:T(8,128)S(1)} %get-tuple-element.267, f32[8,512,128]{1,2,0:T(8,128)} %fusion.19), kind=kOutput, calls=%fused_computation.25 | convolution fusion | flops 807534080 | bytes 5785632 | tf_op jit(solution)/shard_map/bthd,bhde->bthe/dot_general | solution.py:94
  161.7 3.0 copy.98
  164.8 1.9 multiply_reduce_fusion
  166.7 13.4 %all-reduce = (f32[512]{0:T(512)S(1)}, f32[512]{0:T(512)S(1)}) all-reduce(f32[512]{0:T(512)S(1)} %get-tuple-element.277, f32[512]{0:T(512)S(1)} %multiply_reduce_fusion), channel_id=1, replica_groups=mesh['seq'=32,'head'=8] {'head'}, use_global_device_ids=true, to_apply=%region_5.6 | all-reduce | flops 1024 | bytes 8192 | tf_op jit(solution)/shard_map/psum | solution.py:99
  180.1 3.5 multiply_convert_fusion.2
  185.1 3.2 fusion.16
  188.3 3.2 multiply_convert_fusion
  193.4 2.2 fusion.5
  195.6 2.3 copy.112
  197.9 4.4 %fusion.46 = f32[8,128,512]{2,1,0:T(8,128)} fusion(bf16[512,8,128]{0,2,1:T(8,128)(2,1)S(1)} %bitcast.160, bf16[8,512,512]{2,1,0:T(8,128)(2,1)} %copy-done.1), kind=kOutput, calls=%fused_computation.68 | convolution fusion | flops 536870912 | bytes 7340032 | tf_op jit(solution)/shard_map/while/body/eval_jaxpr/hts,thd->shd/dot_general | solution.py:136
  202.3 2.1 fusion.47
  204.4 154.9 %all-gather.8.cloned.1.call-done = f32[256,128,128]{2,1,0:T(8,128)} async-done(((f32[8,128,128]{2,1,0:T(8,128)}), f32[256,128,128]{2,1,0:T(8,128)}) %all-gather.8.cloned.1.call-update) | async-done | bytes 16777232 | tf_op jit(solution)/shard_map/all_gather | solution.py:19
  359.3 38.3 %while.17 = (s32[]{:T(128)}, f32[8,128,128]{2,1,0:T(8,128)S(1)}, s32[]{:T(128)}, f32[32,8]{1,0:T(8,128)S(1)}, f32[32,8,128,128]{3,2,1,0:T(8,128)}, /*index=5*/s32[]{:T(128)}, s32[]{:T(128)}, s32[]{:T(128)}, s32[]{:T(128)}) while((s32[]{:T(128)}, f32[8,128,128]{2,1,0:T(8,128)S(1)}, s32[]{:T(128)}, f32[32,8]{1,0:T(8,128)S(1)}, ...), condition=%wide.region_9.10_spmd, body=%wide.region_8.9_spmd.sunk | while | flops 262150 | bytes 1573115 | solution.py:28
  397.7 3.7 fusion.1
  401.4 2.3 copy.114
  403.6 2.7 fusion.3
  (106 shorter events, 45.3 us)
Async XLA Ops:
  7.2 5.1 %copy-start = (bf16[512,1024]{1,0:T(8,128)(2,1)S(1)}, bf16[512,1024]{1,0:T(8,128)(2,1)}, u32[]{:S(2)}) copy-start(bf16[512,1024]{1,0:T(8,128)(2,1)} %param.12) | copy-start | bytes 3145732
  7.2 150.2 %all-gather.6.cloned.1.call-start = ((), (), s32[]{:S(2)}) async-start(), calls=%async_computation | async-start | bytes 17301504 | tf_op jit(solution)/shard_map/all_gather | solution.py:19
  12.3 2.2 copy-start.8
  14.4 344.9 %all-gather.8.cloned.1.call-start = ((), (), s32[]{:S(2)}) async-start(), calls=%async_computation.1 | async-start | bytes 17301504 | tf_op jit(solution)/shard_map/all_gather | solution.py:19
  16.0 141.4 %copy-start.4 = (bf16[512,1024]{0,1:T(8,128)(2,1)}, bf16[512,1024]{0,1:T(8,128)(2,1)S(1)}, u32[]{:S(2)}) copy-start(bf16[512,1024]{0,1:T(8,128)(2,1)S(1)} %copy.119) | copy-start | bytes 3145732
  57.8 1.9 copy-start.1
  161.7 3.0 copy-start.6
  161.7 3.0 copy-start.10
  188.3 3.2 copy-start.9
  191.5 2.0 copy-start.2
  197.9 4.4 %copy-start.3 = (bf16[8,512,512]{2,1,0:T(8,128)(2,1)S(1)}, bf16[8,512,512]{2,1,0:T(8,128)(2,1)}, u32[]{:S(2)}) copy-start(bf16[8,512,512]{2,1,0:T(8,128)(2,1)} %copy-done.2) | copy-start | bytes 12582916
  197.9 4.4 %copy-start.5 = (bf16[512,1024]{0,1:T(8,128)(2,1)S(1)}, bf16[512,1024]{0,1:T(8,128)(2,1)}, u32[]{:S(2)}) copy-start(bf16[512,1024]{0,1:T(8,128)(2,1)} %copy-done.4) | copy-start | bytes 3145732
  359.3 38.3 %copy-start.7 = (bf16[512,1024]{1,0:T(8,128)(2,1)S(1)}, bf16[512,1024]{1,0:T(8,128)(2,1)}, u32[]{:S(2)}) copy-start(bf16[512,1024]{1,0:T(8,128)(2,1)} %param.11) | copy-start | bytes 3145732
Sparse Core Ops, SparseCore 0:
  14.5 142.8 all-gather.5
  188.4 170.8 all-gather.7
where the time goes:
time: 417 us; the launch traced here: 414 us
  waiting for transfers between devices  250 us (60%)
  blocking collectives  50.7 us (12%)
  other arithmetic  45.1 us (11%)
  matrix products  36.3 us (9%)
  local copies, waits for them, and re-layouts  17.3 us (4%)
  between operations  14.3 us (3%)
    all_gather x2, waiting for transfers between devices, prefix(): gathered = jax.tree.map(lambda a: lax.all_gather(a, axis), part)  250 us
    all_gather x1, blocking collectives, prefix(): gathered = jax.tree.map(lambda a: lax.all_gather(a, axis), part)  37.4 us
    add x31, other arithmetic, chain_combine(): jnp.exp(later[0])[:, None, None] * earlier[1] + later[1]  37 us
    psum x1, blocking collectives, on_device(): lax.psum((jnp.sum(flat_out * flat_out, axis=1), jnp.sum(scaled_grad * fla...  13.4 us
    unnamed x26, local copies, waits for them, and re-layouts  9.79 us
  transfers between devices with their start and end apart: 2, of which 2 were waited for; matrix products, arithmetic and copies ran while one was open for 6% of the time, Pallas kernels for 0%

commit v1 on v0

v1 whole, which is shorter than its diff:
```python
import functools

import jax
import jax.numpy as jnp
from jax import lax
from jax.experimental import pallas as pl
from jax.experimental.pallas import tpu as pltpu
from jax.sharding import PartitionSpec as P

DIM = 128
BLOCK = 512
HALF = 256
EPSILON = 1e-06
F32 = jnp.float32
BF16 = jnp.bfloat16
NN = (((1,), (0,)), ((), ()))
NT = (((1,), (1,)), ((), ()))
TN = (((0,), (0,)), ((), ()))


def mul(a, b, dims):
    return lax.dot_general(a, b, dims, preferred_element_type=F32)


def split(x):
    high = x.astype(BF16)
    return high, (x - high.astype(F32)).astype(BF16)


def kernel(
    seq_count, head_count, heads,
    log_ref, gain_ref, query_hbm, key_hbm, value_hbm, cot_hbm,
    att_hbm, gq_hbm, gk_hbm, gv_hbm,
    query, key, value, cot, att, gq, gk, gv,
    cum_row, cum_col, decay0, decay1, weight0, weight1,
    out, grad, inner_key, inner_value,
    own_total, totals,
    piece, arrived, before, state,
    grad_piece, grad_arrived, after, after_state,
    stat, stats,
    in_sem, out_sem, total_sem, first_sem, second_sem, stat_sem, third_sem, fourth_sem,
):
    me = lax.axis_index("seq")
    place = lax.axis_index("head")
    rows = piece.shape[1]
    parts = DIM // rows
    features = head_count * heads * DIM

    loads = [
        pltpu.make_async_copy(source, target, in_sem.at[i])
        for i, (source, target) in enumerate(
            ((key_hbm, key), (value_hbm, value), (query_hbm, query), (cot_hbm, cot))
        )
    ]
    for load in loads:
        load.start()

    barrier = pltpu.get_barrier_semaphore()

    def greet_seq(d, carry):
        pl.semaphore_signal(
            barrier, inc=1, device_id={"seq": lax.rem(me + d, seq_count)},
            device_id_type=pl.DeviceIdType.MESH,
        )
        return carry

    def greet_head(d, carry):
        pl.semaphore_signal(
            barrier, inc=1, device_id={"head": lax.rem(place + d, head_count)},
            device_id_type=pl.DeviceIdType.MESH,
        )
        return carry

    lax.fori_loop(1, seq_count, greet_seq, 0)
    lax.fori_loop(1, head_count, greet_head, 0)

    def columns(h):
        return pl.ds(pl.multiple_of(h * DIM, DIM), DIM)

    def exchange(source, target, send, receive, axis, mine, count, same):
        own = source if same else source.at[mine]
        pltpu.make_async_copy(own, target.at[mine], receive).start()

        def one(d, carry):
            peer = lax.rem(mine + d, count)
            pltpu.make_async_remote_copy(
                src_ref=source if same else source.at[peer],
                dst_ref=target.at[mine],
                send_sem=send,
                recv_sem=receive,
                device_id={axis: peer},
                device_id_type=pl.DeviceIdType.MESH,
            ).start()
            return carry

        lax.fori_loop(1, count, one, 0)

    def arrive(target, receive):
        pltpu.make_async_copy(target, target, receive).wait()

    def sent(target, send, count):
        some = target.at[pl.ds(0, count - 1)]
        pltpu.make_async_copy(some, some, send).wait()

    lower = lax.broadcasted_iota(jnp.int32, (BLOCK, BLOCK), 0) >= lax.broadcasted_iota(
        jnp.int32, (BLOCK, BLOCK), 1
    )
    cumulative = lax.dot_general(
        log_ref[...], lower.astype(F32), NT,
        precision=lax.Precision.HIGHEST, preferred_element_type=F32,
    )
    cum_row[...] = cumulative
    turned = jnp.transpose(jnp.concatenate([cumulative] * (DIM // heads), axis=0))
    for h in range(heads):
        spread = jnp.broadcast_to(turned[:, h : h + 1], (BLOCK, DIM))
        cum_col[:, h * DIM : (h + 1) * DIM] = spread
        for part in range(parts):
            own_total[part * heads + h] = spread[BLOCK - 1 :, :]

    pl.semaphore_wait(barrier, seq_count + head_count - 2)
    exchange(own_total, totals, total_sem.at[0], total_sem.at[1], "seq", me, seq_count, False)

    loads[0].wait()
    loads[1].wait()

    def store_piece(target, h, result):
        for part in range(parts):
            target[part * heads + h] = result[part * rows : (part + 1) * rows]

    def load_state(source, h):
        return jnp.concatenate([source[part * heads + h] for part in range(parts)], axis=0)

    def make_piece(h, carry):
        at = columns(h)
        cum = cum_col[:, at]
        trail = jnp.exp(own_total[h] - cum)
        high, low = split(key[:, at].astype(F32) * trail)
        both = value[:, at]
        store_piece(piece, h, mul(high, both, TN) + mul(low, both, TN))
        return carry

    lax.fori_loop(0, heads, make_piece, 0)
    exchange(piece, arrived, first_sem.at[0], first_sem.at[1], "seq", me, seq_count, False)

    loads[2].wait()
    loads[3].wait()
    causal = lax.broadcasted_iota(jnp.int32, (HALF, HALF), 0) >= lax.broadcasted_iota(
        jnp.int32, (HALF, HALF), 1
    )

    def forward(h, carry):
        at = columns(h)
        row = cum_row[pl.ds(h, 1), :]
        top = cum_col[:HALF, at]
        top = jnp.concatenate([top, top], axis=1)
        low = cum_col[HALF:, at]
        low = jnp.concatenate([low, low], axis=1)
        left, right = row[:, :HALF], row[:, HALF:]
        masked = -1e30
        d0 = jnp.exp(jnp.where(causal, top - left, masked))
        d1 = jnp.concatenate(
            [jnp.exp(low - left), jnp.exp(jnp.where(causal, low - right, masked))], axis=1
        )
        decay0[h] = d0
        decay1[h] = d1
        keys = key[:, at]
        values = value[:, at]
        w0 = (mul(query[:HALF, at], keys[:HALF], NT) * d0).astype(BF16)
        w1 = (mul(query[HALF:, at], keys, NT) * d1).astype(BF16)
        weight0[h] = w0
        weight1[h] = w1
        out[:HALF, at] = mul(w0, values[:HALF], NN)
        out[HALF:, at] = mul(w1, values, NN)
        return carry

    lax.fori_loop(0, heads, forward, 0)

    arrive(totals, total_sem.at[1])
    arrive(arrived, first_sem.at[1])

    def advance(b, running):
        before[b] = running
        return jnp.exp(totals[b]) * running + arrived[b]

    lax.fori_loop(0, seq_count, advance, jnp.zeros((rows, DIM), F32))
    exchange(before, state, second_sem.at[0], second_sem.at[1], "seq", me, seq_count, False)
    arrive(state, second_sem.at[1])

    def finish_out(h, carry):
        squares, inners = carry
        at = columns(h)
        lead = jnp.exp(cum_col[:, at])
        high, low = split(load_state(state, h))
        outer = mul(query[:, at], jnp.concatenate([high, low], axis=1), NN)
        whole = out[:, at] + lead * (outer[:, :DIM] + outer[:, DIM:])
        out[:, at] = whole
        scaled = cot[:, at].astype(F32) * gain_ref[:, at]
        return squares + whole * whole, inners + scaled * whole

    zero = jnp.zeros((BLOCK, DIM), F32)
    squares, inners = lax.fori_loop(0, heads, finish_out, (zero, zero))
    square_row = jnp.sum(jnp.transpose(squares), axis=0, keepdims=True)
    inner_row = jnp.sum(jnp.transpose(inners), axis=0, keepdims=True)
    for i in range(BLOCK // DIM):
        stat[i : i + 1, :] = square_row[:, i * DIM : (i + 1) * DIM]
        stat[4 + i : 5 + i, :] = inner_row[:, i * DIM : (i + 1) * DIM]
    exchange(stat, stats, stat_sem.at[0], stat_sem.at[1], "head", place, head_count, True)
    arrive(stats, stat_sem.at[1])
    summed = stats[0]
    for i in range(1, head_count):
        summed = summed + stats[i]
    inverse_rows = lax.rsqrt(summed[:4] / features + EPSILON)
    mean_rows = inverse_rows * summed[4:] / features

    def to_columns(four):
        return jnp.concatenate(
            [jnp.transpose(jnp.broadcast_to(four[i : i + 1], (DIM, DIM))) for i in range(4)], axis=0
        )

    inverse = to_columns(inverse_rows)
    mean_term = to_columns(mean_rows)

    def make_grad(h, carry):
        at = columns(h)
        gain = gain_ref[:, at]
        normed = out[:, at] * inverse
        att[:, at] = (normed * gain).astype(BF16)
        scaled = cot[:, at].astype(F32) * gain
        g = (inverse * (scaled - normed * mean_term)).astype(BF16)
        grad[:, at] = g
        high, low = split(query[:, at].astype(F32) * jnp.exp(cum_col[:, at]))
        store_piece(grad_piece, h, mul(high, g, TN) + mul(low, g, TN))
        return carry

    lax.fori_loop(0, heads, make_grad, 0)
    exchange(grad_piece, grad_arrived, third_sem.at[0], third_sem.at[1], "seq", me, seq_count, False)
    store_att = pltpu.make_async_copy(att, att_hbm, out_sem.at[0])
    store_att.start()

    def backward(h, carry):
        at = columns(h)
        d0 = decay0[h]
        d1 = decay1[h]
        keys = key[:, at]
        values = value[:, at]
        g = grad[:, at]
        q = query[:, at]
        w0 = weight0[h]
        w1 = weight1[h]
        g0 = (mul(g[:HALF], values[:HALF], NT) * d0).astype(BF16)
        g1 = (mul(g[HALF:], values, NT) * d1).astype(BF16)
        high, low = split(load_state(state, h))
        outer = mul(g, high, NT) + mul(g, low, NT)
        lead = jnp.exp(cum_col[:, at])
        gq[:HALF, at] = (mul(g0, keys[:HALF], NN) + lead[:HALF] * outer[:HALF]).astype(BF16)
        gq[HALF:, at] = (mul(g1, keys, NN) + lead[HALF:] * outer[HALF:]).astype(BF16)
        full_key = mul(g1, q[HALF:], TN)
        full_value = mul(w1, g[HALF:], TN)
        inner_key[:HALF, at] = full_key[:HALF] + mul(g0, q[:HALF], TN)
        inner_key[HALF:, at] = full_key[HALF:]
        inner_value[:HALF, at] = full_value[:HALF] + mul(w0, g[:HALF], TN)
        inner_value[HALF:, at] = full_value[HALF:]
        return carry

    lax.fori_loop(0, heads, backward, 0)
    store_gq = pltpu.make_async_copy(gq, gq_hbm, out_sem.at[1])
    store_gq.start()
    arrive(grad_arrived, third_sem.at[1])

    def retreat(turn, running):
        b = seq_count - 1 - turn
        after[b] = running
        return grad_arrived[b] + jnp.exp(totals[b]) * running

    lax.fori_loop(0, seq_count, retreat, jnp.zeros((rows, DIM), F32))
    exchange(after, after_state, fourth_sem.at[0], fourth_sem.at[1], "seq", me, seq_count, False)
    arrive(after_state, fourth_sem.at[1])

    def finish(h, carry):
        at = columns(h)
        high, low = split(load_state(after_state, h))
        trail = jnp.exp(own_total[h] - cum_col[:, at])
        values = value[:, at]
        from_value = mul(values, high, NT) + mul(values, low, NT)
        gk[:, at] = (inner_key[:, at] + trail * from_value).astype(BF16)
        from_key = mul(key[:, at], jnp.concatenate([high, low], axis=1), NN)
        gv[:, at] = (
            inner_value[:, at] + trail * (from_key[:, :DIM] + from_key[:, DIM:])
        ).astype(BF16)
        return carry

    lax.fori_loop(0, heads, finish, 0)
    store_gk = pltpu.make_async_copy(gk, gk_hbm, out_sem.at[2])
    store_gv = pltpu.make_async_copy(gv, gv_hbm, out_sem.at[3])
    store_gk.start()
    store_gv.start()

    sent(totals, total_sem.at[0], seq_count)
    sent(arrived, first_sem.at[0], seq_count)
    sent(state, second_sem.at[0], seq_count)
    sent(stats, stat_sem.at[0], head_count)
    sent(grad_arrived, third_sem.at[0], seq_count)
    sent(after_state, fourth_sem.at[0], seq_count)
    store_att.wait()
    store_gq.wait()
    store_gk.wait()
    store_gv.wait()


def on_device(seq_count, head_count, queries, key_vecs, value_vecs, log_decay, norm_gain, cotangent):
    tokens, width = queries.shape
    heads = width // DIM
    rows = heads * DIM // seq_count
    big = jax.ShapeDtypeStruct((tokens, width), BF16)
    vmem = pl.BlockSpec(memory_space=pltpu.VMEM)
    hbm = pl.BlockSpec(memory_space=pl.ANY)
    narrow = pltpu.VMEM((tokens, width), BF16)
    wide = pltpu.VMEM((tokens, width), F32)
    chunk = pltpu.VMEM((seq_count, rows, DIM), F32)
    line = pltpu.VMEM((seq_count, 1, DIM), F32)
    pair = pltpu.SemaphoreType.DMA((2,))
    four = pltpu.SemaphoreType.DMA((4,))
    return pl.pallas_call(
        functools.partial(kernel, seq_count, head_count, heads),
        out_shape=(big,) * 4,
        in_specs=[vmem, vmem] + [hbm] * 4,
        out_specs=(hbm,) * 4,
        scratch_shapes=[narrow] * 8
        + [
            pltpu.VMEM((heads, tokens), F32),
            wide,
            pltpu.VMEM((heads, HALF, HALF), F32),
            pltpu.VMEM((heads, HALF, BLOCK), F32),
            pltpu.VMEM((heads, HALF, HALF), BF16),
            pltpu.VMEM((heads, HALF, BLOCK), BF16),
            wide,
            narrow,
            wide,
            wide,
            line,
            line,
        ]
        + [chunk] * 8
        + [pltpu.VMEM((8, DIM), F32), pltpu.VMEM((head_count, 8, DIM), F32)]
        + [four, four]
        + [pair] * 6,
        compiler_params=pltpu.CompilerParams(
            collective_id=0, has_side_effects=True, vmem_limit_bytes=60 * 1024 * 1024
        ),
    )(log_decay.T, norm_gain.reshape(1, width), queries, key_vecs, value_vecs, cotangent)


def solution(mesh):
    return jax.shard_map(
        functools.partial(on_device, mesh.shape["seq"], mesh.shape["head"]),
        mesh=mesh,
        in_specs=(
            P("seq", "head"),
            P("seq", "head"),
            P("seq", "head"),
            P("seq", "head"),
            P("head"),
            P("seq", "head"),
        ),
        out_specs=(P("seq", "head"), P("seq", "head"), P("seq", "head"), P("seq", "head")),
        check_vma=False,
    )
```

time: 417 us -> 91.9 us (0.22)
  waiting for transfers between devices: 250 us -> 0 us
  Pallas kernels: 0 us -> 83.2 us
  blocking collectives: 50.7 us -> 0 us
  other arithmetic: 45.1 us -> 0 us
  matrix products: 36.3 us -> 0 us
  between operations: 14.3 us -> 0.65 us
  local copies, waits for them, and re-layouts: 17.3 us -> 6.53 us
    all_gather x2 -> x0, waiting for transfers between devices: 250 us -> none  [prefix(): gathered = jax.tree.map(lambda a: lax.all_gather(a, axis), part)]
    pallas_call x0 -> x1, Pallas kernels: none -> 83.2 us  [on_device(): pl.pallas_call(functools.partial(kernel, seq_count, head_count, heads), o...]
    all_gather x1 -> x0, blocking collectives: 37.4 us -> none  [prefix(): gathered = jax.tree.map(lambda a: lax.all_gather(a, axis), part)]
    add x31 -> x0, other arithmetic: 37 us -> none  [chain_combine(): jnp.exp(later[0])[:, None, None] * earlier[1] + later[1]]
    dot_general x12 -> x0, matrix products: 36.3 us -> none  [the longest x1 4.41 us: backward_inner(): jnp.einsum('hts,thd->shd', weights, grad_block, preferred_element_type=jn...]
    psum x1 -> x0, blocking collectives: 13.4 us -> none  [on_device(): lax.psum((jnp.sum(flat_out * flat_out, axis=1), jnp.sum(scaled_grad * fla...]
    unnamed x26 -> x10, local copies, waits for them, and re-layouts: 9.79 us -> 6.53 us
  transfers between devices with their start and end apart: 2 -> 0, of which waited for: 2 -> 0; matrix products, arithmetic and copies ran while one was open for 6% -> 0% of each run, Pallas kernels for 0% -> 0%
where the time goes in v1:
time: 91.9 us; the launch traced here: 90.4 us
  Pallas kernels  83.2 us (91%)
  local copies, waits for them, and re-layouts  6.53 us (7%)
    pallas_call x1, Pallas kernels, on_device(): pl.pallas_call(functools.partial(kernel, seq_count, head_count, heads), o...  83.2 us
    unnamed x10, local copies, waits for them, and re-layouts  6.53 us

profile of v1, /device:TPU:1, one launch (start us, length us, event | category | flops | bytes accessed | tf_op | source)
XLA Modules:
  0.0 90.4 jit_solution(7723377601030702281)
XLA Ops:
  0.6 83.2 %shard_map.93 = (bf16[512,1024]{1,0:T(8,128)(2,1)}, bf16[512,1024]{1,0:T(8,128)(2,1)}, bf16[512,1024]{1,0:T(8,128)(2,1)}, bf16[512,1024]{1,0:T(8,128)(2,1)}) custom-call(f32[8,512]{1,0:T(8,128)} %bitcast.2, f32[1,1024]{1,0:T(1,128)} %bitcast.3, bf16[512,1024]{1,0:T(8,128)(2,1)} %query_hbm.1, bf16[512,1024]{1,0:T(8,128)(2,1)} %key_hbm.1, ...), custom_call_target="tpu_custom_call" | custom-call | tf_op jit(solution)/shard_map/pallas_call | solution.py:323
  83.9 0.0 copy-start.2
  83.9 2.4 %copy.14 = bf16[512,1024]{1,0:T(8,128)(2,1)} copy(bf16[512,1024]{1,0:T(8,128)(2,1)} %get-tuple-element.8) | data formatting | bytes 2097152
  86.2 0.0 copy-done.2
  86.2 0.0 copy-start.1
  86.2 1.0 %copy.15 = bf16[512,1024]{1,0:T(8,128)(2,1)} copy(bf16[512,1024]{1,0:T(8,128)(2,1)S(1)} %copy-done.2) | data formatting | bytes 2097152
  87.2 0.6 copy-done.1
  87.8 0.0 copy-start
  87.9 1.0 %copy.16 = bf16[512,1024]{1,0:T(8,128)(2,1)} copy(bf16[512,1024]{1,0:T(8,128)(2,1)S(1)} %copy-done.1) | data formatting | bytes 2097152
  88.8 0.6 copy-done
  89.5 1.0 %copy.17 = bf16[512,1024]{1,0:T(8,128)(2,1)} copy(bf16[512,1024]{1,0:T(8,128)(2,1)S(1)} %copy-done) | data formatting | bytes 2097152
Async XLA Ops:
  83.9 2.4 %copy-start.2 = (bf16[512,1024]{1,0:T(8,128)(2,1)S(1)}, bf16[512,1024]{1,0:T(8,128)(2,1)}, u32[]{:S(2)}) copy-start(bf16[512,1024]{1,0:T(8,128)(2,1)} %get-tuple-element.9) | copy-start | bytes 3145732
  86.2 1.6 %copy-start.1 = (bf16[512,1024]{1,0:T(8,128)(2,1)S(1)}, bf16[512,1024]{1,0:T(8,128)(2,1)}, u32[]{:S(2)}) copy-start(bf16[512,1024]{1,0:T(8,128)(2,1)} %get-tuple-element.10) | copy-start | bytes 3145732
  87.8 1.6 %copy-start = (bf16[512,1024]{1,0:T(8,128)(2,1)S(1)}, bf16[512,1024]{1,0:T(8,128)(2,1)}, u32[]{:S(2)}) copy-start(bf16[512,1024]{1,0:T(8,128)(2,1)} %get-tuple-element.11) | copy-start | bytes 3145732

commit v2 on v1

v2 whole, which is shorter than its diff:
```python
import functools

import jax
import jax.numpy as jnp
from jax import lax
from jax.experimental import pallas as pl
from jax.experimental.pallas import tpu as pltpu
from jax.sharding import PartitionSpec as P

DIM = 128
BLOCK = 512
HALF = 256
EPSILON = 1e-06
F32 = jnp.float32
BF16 = jnp.bfloat16
NN = (((1,), (0,)), ((), ()))
NT = (((1,), (1,)), ((), ()))
TN = (((0,), (0,)), ((), ()))


def mul(a, b, dims):
    return lax.dot_general(a, b, dims, preferred_element_type=F32)


def split(x):
    high = x.astype(BF16)
    return high, (x - high.astype(F32)).astype(BF16)


def store_kernel(*refs):
    sources, targets, sem = refs[:4], refs[4:8], refs[8]
    copies = [
        pltpu.make_async_copy(source, target, sem.at[i])
        for i, (source, target) in enumerate(zip(sources, targets))
    ]
    for copy in copies:
        copy.start()
    for copy in copies:
        copy.wait()


def kernel(
    planes, plane_size, head_count, heads, early, early_back,
    log_ref, gain_ref, query_hbm, key_hbm, value_hbm, cot_hbm,
    att, gq, gk, gv,
    query, key, value, cot,
    cum_row, cum_col, lead, trail, decay0, decay1, weight0, weight1,
    out, scaled, query_high, query_low, grad, inner_key, inner_value,
    own_total, totals,
    piece, arrived, before, state,
    grad_piece, grad_arrived, after, after_state,
    stat, stats,
    in_sem, total_sem, stat_sem, give_send, give_receive, take_send, take_receive,
):
    me = lax.axis_index("seq")
    plane = me // plane_size
    spot = lax.rem(me, plane_size)
    place = lax.axis_index("head")
    seq_count = planes * plane_size
    rows = piece.shape[1]
    half_rows = rows // 2
    features = head_count * heads * DIM

    loads = [
        pltpu.make_async_copy(source, target, in_sem.at[i])
        for i, (source, target) in enumerate(
            ((key_hbm, key), (value_hbm, value), (query_hbm, query), (cot_hbm, cot))
        )
    ]
    for load in loads:
        load.start()

    barrier = pltpu.get_barrier_semaphore()

    def greet_seq(d, carry):
        pl.semaphore_signal(
            barrier, inc=1, device_id={"seq": lax.rem(me + d, seq_count)},
            device_id_type=pl.DeviceIdType.MESH,
        )
        return carry

    def greet_head(d, carry):
        pl.semaphore_signal(
            barrier, inc=1, device_id={"head": lax.rem(place + d, head_count)},
            device_id_type=pl.DeviceIdType.MESH,
        )
        return carry

    lax.fori_loop(1, seq_count, greet_seq, 0)
    lax.fori_loop(1, head_count, greet_head, 0)

    def columns(h):
        return pl.ds(pl.multiple_of(h * DIM, DIM), DIM)

    def turn_of(i):
        return plane_size // 2 + (1 - 2 * lax.rem(i, 2)) * ((i + 1) // 2)

    def part_rows(part):
        return pl.ds(part * half_rows, half_rows)

    def slots(h):
        return pl.ds(pl.multiple_of(h * planes, planes), planes)

    def remote(source, target, send, receive, peer):
        pltpu.make_async_remote_copy(
            src_ref=source, dst_ref=target, send_sem=send, recv_sem=receive,
            device_id=peer, device_id_type=pl.DeviceIdType.MESH,
        ).start()

    def give_head(source, target, which, part, h, own):
        at = part_rows(part)
        for d in range(planes):
            p = lax.rem(plane + d, planes)
            if own and d == 0:
                pltpu.make_async_copy(
                    source.at[h * planes + p, at], target.at[me, at], give_receive.at[which, part]
                ).start()
            else:
                remote(
                    source.at[h * planes + p, at], target.at[me, at],
                    give_send.at[which, part], give_receive.at[which, part],
                    {"seq": p * plane_size + h},
                )

    def give_all(source, target, which, part):
        def one(i, carry):
            give_head(source, target, which, part, lax.rem(spot + turn_of(i), plane_size), False)
            return carry

        lax.fori_loop(0, plane_size - 1, one, 0)
        give_head(source, target, which, part, spot, True)

    def take_all(source, target, which, part):
        at = part_rows(part)
        slot = spot * planes + plane

        def one_spot(z, own):
            for d in range(planes):
                p = lax.rem(plane + d, planes)
                b = p * plane_size + z
                if own and d == 0:
                    pltpu.make_async_copy(
                        source.at[b, at], target.at[slot, at], take_receive.at[which, spot]
                    ).start()
                else:
                    remote(
                        source.at[b, at], target.at[slot, at],
                        take_send.at[which, part], take_receive.at[which, spot], {"seq": b},
                    )

        def one(i, carry):
            one_spot(lax.rem(spot + turn_of(i), plane_size), False)
            return carry

        lax.fori_loop(0, plane_size - 1, one, 0)
        one_spot(spot, True)

    def given(target, which, part):
        some = target.at[:, part_rows(part)]
        pltpu.make_async_copy(some, some, give_receive.at[which, part]).wait()

    def taken(target, which, h):
        some = target.at[slots(h)]
        pltpu.make_async_copy(some, some, take_receive.at[which, h]).wait()

    def sent(target, send):
        some = target.at[pl.ds(0, seq_count - 1), part_rows(0)]
        pltpu.make_async_copy(some, some, send).wait()

    def store_piece(target, h, result):
        target[slots(h)] = result.reshape(planes, rows, DIM)

    def load_state(source, h):
        return source[slots(h)].reshape(DIM, DIM)

    lower = lax.broadcasted_iota(jnp.int32, (BLOCK, BLOCK), 0) >= lax.broadcasted_iota(
        jnp.int32, (BLOCK, BLOCK), 1
    )
    cumulative = lax.dot_general(
        log_ref[...], lower.astype(F32), NT,
        precision=lax.Precision.HIGHEST, preferred_element_type=F32,
    )
    cum_row[...] = cumulative
    turned = jnp.transpose(jnp.concatenate([cumulative] * (DIM // heads), axis=0))
    for h in range(heads):
        spread = jnp.broadcast_to(turned[:, h : h + 1], (BLOCK, DIM))
        cum_col[:, h * DIM : (h + 1) * DIM] = spread
        total = spread[BLOCK - 1 :, :]
        trail[:, h * DIM : (h + 1) * DIM] = jnp.exp(total - spread)
        for p in range(planes):
            own_total[h * planes + p] = total

    loads[0].wait()
    loads[1].wait()

    def make_piece(h, carry):
        at = columns(h)
        high, low = split(key[:, at].astype(F32) * trail[:, at])
        both = value[:, at]
        store_piece(piece, h, mul(high, both, TN) + mul(low, both, TN))
        return carry

    lax.fori_loop(0, heads, make_piece, 0)
    pl.semaphore_wait(barrier, seq_count + head_count - 2)
    give_all(piece, arrived, 0, 0)

    pltpu.make_async_copy(
        own_total.at[spot * planes + plane], totals.at[me], total_sem.at[1]
    ).start()

    def share_total(d, carry):
        peer = lax.rem(me + d, seq_count)
        slot = lax.rem(peer, plane_size) * planes + peer // plane_size
        remote(own_total.at[slot], totals.at[me], total_sem.at[0], total_sem.at[1], {"seq": peer})
        return carry

    lax.fori_loop(1, seq_count, share_total, 0)
    give_all(piece, arrived, 0, 1)

    loads[2].wait()
    loads[3].wait()
    causal = lax.broadcasted_iota(jnp.int32, (HALF, HALF), 0) >= lax.broadcasted_iota(
        jnp.int32, (HALF, HALF), 1
    )

    def forward(h, carry):
        at = columns(h)
        row = cum_row[pl.ds(h, 1), :]
        col = cum_col[:, at]
        top = jnp.concatenate([col[:HALF]] * 2, axis=1)
        low = jnp.concatenate([col[HALF:]] * 2, axis=1)
        left, right = row[:, :HALF], row[:, HALF:]
        masked = -1e30
        d0 = jnp.exp(jnp.where(causal, top - left, masked))
        d1 = jnp.concatenate(
            [jnp.exp(low - left), jnp.exp(jnp.where(causal, low - right, masked))], axis=1
        )
        decay0[h] = d0
        decay1[h] = d1
        keys = key[:, at]
        values = value[:, at]
        w0 = (mul(query[:HALF, at], keys[:HALF], NT) * d0).astype(BF16)
        w1 = (mul(query[HALF:, at], keys, NT) * d1).astype(BF16)
        weight0[h] = w0
        weight1[h] = w1
        out[:HALF, at] = mul(w0, values[:HALF], NN)
        out[HALF:, at] = mul(w1, values, NN)
        return carry

    def advance(part):
        at = part_rows(part)

        def one(b, running):
            before[b, at] = running
            return jnp.exp(totals[b]) * running + arrived[b, at]

        lax.fori_loop(0, seq_count, one, jnp.zeros((half_rows, DIM), F32))

    def prepare(h, carry):
        at = columns(h)
        grown = jnp.exp(cum_col[:, at])
        lead[:, at] = grown
        high, low = split(query[:, at].astype(F32) * grown)
        query_high[:, at] = high
        query_low[:, at] = low
        scaled[:, at] = cot[:, at].astype(F32) * gain_ref[:, at]
        return carry

    lax.fori_loop(0, early, forward, 0)
    pltpu.make_async_copy(totals, totals, total_sem.at[1]).wait()
    given(arrived, 0, 0)
    advance(0)
    take_all(before, state, 0, 0)
    lax.fori_loop(early, heads, forward, 0)
    given(arrived, 0, 1)
    advance(1)
    take_all(before, state, 0, 1)
    lax.fori_loop(0, heads, prepare, 0)

    def finish_out(i, carry):
        squares, inners = carry
        h = lax.rem(spot + plane_size - turn_of(i), plane_size)
        taken(state, 0, h)
        at = columns(h)
        high, low = split(load_state(state, h))
        outer = mul(query[:, at], jnp.concatenate([high, low], axis=1), NN)
        whole = out[:, at] + lead[:, at] * (outer[:, :DIM] + outer[:, DIM:])
        out[:, at] = whole
        return squares + whole * whole, inners + scaled[:, at] * whole

    zero = jnp.zeros((BLOCK, DIM), F32)
    squares, inners = lax.fori_loop(0, heads, finish_out, (zero, zero))
    square_row = jnp.sum(jnp.transpose(squares), axis=0, keepdims=True)
    inner_row = jnp.sum(jnp.transpose(inners), axis=0, keepdims=True)
    for i in range(BLOCK // DIM):
        stat[i : i + 1, :] = square_row[:, i * DIM : (i + 1) * DIM]
        stat[4 + i : 5 + i, :] = inner_row[:, i * DIM : (i + 1) * DIM]
    pltpu.make_async_copy(stat, stats.at[place], stat_sem.at[1]).start()

    def share_stat(d, carry):
        peer = lax.rem(place + d, head_count)
        remote(stat, stats.at[place], stat_sem.at[0], stat_sem.at[1], {"head": peer})
        return carry

    lax.fori_loop(1, head_count, share_stat, 0)
    pltpu.make_async_copy(stats, stats, stat_sem.at[1]).wait()
    summed = stats[0]
    for i in range(1, head_count):
        summed = summed + stats[i]
    inverse_rows = lax.rsqrt(summed[:4] / features + EPSILON)
    mean_rows = inverse_rows * summed[4:] / features

    def to_columns(four):
        return jnp.concatenate(
            [jnp.transpose(jnp.broadcast_to(four[i : i + 1], (DIM, DIM))) for i in range(4)], axis=0
        )

    inverse = to_columns(inverse_rows)
    mean_term = to_columns(mean_rows)

    def make_grad(i, carry):
        h = lax.rem(spot + turn_of(i), plane_size)
        at = columns(h)
        normed = out[:, at] * inverse
        out[:, at] = normed
        g = (inverse * (scaled[:, at] - normed * mean_term)).astype(BF16)
        grad[:, at] = g
        store_piece(
            grad_piece, h, mul(query_high[:, at], g, TN) + mul(query_low[:, at], g, TN)
        )
        return h

    def make_and_give(i, carry):
        give_head(grad_piece, grad_arrived, 1, 0, make_grad(i, carry), False)
        return carry

    lax.fori_loop(0, heads - 1, make_and_give, 0)
    make_grad(heads - 1, 0)
    give_head(grad_piece, grad_arrived, 1, 0, spot, True)
    give_all(grad_piece, grad_arrived, 1, 1)

    def backward(h, carry):
        at = columns(h)
        d0 = decay0[h]
        d1 = decay1[h]
        keys = key[:, at]
        values = value[:, at]
        g = grad[:, at]
        q = query[:, at]
        w0 = weight0[h]
        w1 = weight1[h]
        att[:, at] = (out[:, at] * gain_ref[:, at]).astype(BF16)
        g0 = (mul(g[:HALF], values[:HALF], NT) * d0).astype(BF16)
        g1 = (mul(g[HALF:], values, NT) * d1).astype(BF16)
        high, low = split(load_state(state, h))
        outer = lead[:, at] * (mul(g, high, NT) + mul(g, low, NT))
        gq[:HALF, at] = (mul(g0, keys[:HALF], NN) + outer[:HALF]).astype(BF16)
        gq[HALF:, at] = (mul(g1, keys, NN) + outer[HALF:]).astype(BF16)
        full_key = mul(g1, q[HALF:], TN)
        full_value = mul(w1, g[HALF:], TN)
        inner_key[:HALF, at] = full_key[:HALF] + mul(g0, q[:HALF], TN)
        inner_key[HALF:, at] = full_key[HALF:]
        inner_value[:HALF, at] = full_value[:HALF] + mul(w0, g[:HALF], TN)
        inner_value[HALF:, at] = full_value[HALF:]
        return carry

    def retreat(part):
        at = part_rows(part)

        def one(turn, running):
            b = seq_count - 1 - turn
            after[b, at] = running
            return grad_arrived[b, at] + jnp.exp(totals[b]) * running

        lax.fori_loop(0, seq_count, one, jnp.zeros((half_rows, DIM), F32))

    lax.fori_loop(0, early_back, backward, 0)
    given(grad_arrived, 1, 0)
    retreat(0)
    take_all(after, after_state, 1, 0)
    lax.fori_loop(early_back, early_back + 2, backward, 0)
    given(grad_arrived, 1, 1)
    retreat(1)
    take_all(after, after_state, 1, 1)
    lax.fori_loop(early_back + 2, heads, backward, 0)

    def finish(i, carry):
        h = lax.rem(spot + plane_size - turn_of(i), plane_size)
        taken(after_state, 1, h)
        at = columns(h)
        high, low = split(load_state(after_state, h))
        shrunk = trail[:, at]
        values = value[:, at]
        from_value = mul(values, high, NT) + mul(values, low, NT)
        gk[:, at] = (inner_key[:, at] + shrunk * from_value).astype(BF16)
        from_key = mul(key[:, at], jnp.concatenate([high, low], axis=1), NN)
        gv[:, at] = (
            inner_value[:, at] + shrunk * (from_key[:, :DIM] + from_key[:, DIM:])
        ).astype(BF16)
        return carry

    lax.fori_loop(0, heads, finish, 0)

    some = totals.at[pl.ds(0, seq_count - 1)]
    pltpu.make_async_copy(some, some, total_sem.at[0]).wait()
    some = stats.at[pl.ds(0, head_count - 1)]
    pltpu.make_async_copy(some, some, stat_sem.at[0]).wait()
    for which in range(2):
        for part in range(2):
            sent(piece, give_send.at[which, part])
            sent(piece, take_send.at[which, part])


def on_device(seq_count, head_count, queries, key_vecs, value_vecs, log_decay, norm_gain, cotangent):
    tokens, width = queries.shape
    heads = width // DIM
    rows = heads * DIM // seq_count
    planes = seq_count // heads
    vmem = pl.BlockSpec(memory_space=pltpu.VMEM)
    hbm = pl.BlockSpec(memory_space=pltpu.HBM)
    narrow = pltpu.VMEM((tokens, width), BF16)
    wide = pltpu.VMEM((tokens, width), F32)
    chunk = pltpu.VMEM((seq_count, rows, DIM), F32)
    line = pltpu.VMEM((seq_count, 1, DIM), F32)
    pair = pltpu.SemaphoreType.DMA((2,))
    square = pltpu.SemaphoreType.DMA((2, 2))
    results = pl.pallas_call(
        functools.partial(kernel, planes, heads, head_count, heads, 4, 3),
        out_shape=(narrow,) * 4,
        in_specs=[vmem, vmem] + [hbm] * 4,
        out_specs=(vmem,) * 4,
        scratch_shapes=[narrow] * 4
        + [
            pltpu.VMEM((heads, tokens), F32),
            wide,
            wide,
            wide,
            pltpu.VMEM((heads, HALF, HALF), F32),
            pltpu.VMEM((heads, HALF, BLOCK), F32),
            pltpu.VMEM((heads, HALF, HALF), BF16),
            pltpu.VMEM((heads, HALF, BLOCK), BF16),
            wide,
            wide,
            narrow,
            narrow,
            narrow,
            wide,
            wide,
            line,
            line,
        ]
        + [chunk] * 8
        + [pltpu.VMEM((8, DIM), F32), pltpu.VMEM((head_count, 8, DIM), F32)]
        + [pltpu.SemaphoreType.DMA((4,)), pair, pair, square, square, square]
        + [pltpu.SemaphoreType.DMA((2, heads))],
        compiler_params=pltpu.CompilerParams(
            collective_id=0, has_side_effects=True, vmem_limit_bytes=59 * 1024 * 1024
        ),
    )(log_decay.T, norm_gain.reshape(1, width), queries, key_vecs, value_vecs, cotangent)
    return pl.pallas_call(
        store_kernel,
        out_shape=(jax.ShapeDtypeStruct((tokens, width), BF16),) * 4,
        in_specs=[vmem] * 4,
        out_specs=(hbm,) * 4,
        scratch_shapes=[pltpu.SemaphoreType.DMA((4,))],
        compiler_params=pltpu.CompilerParams(vmem_limit_bytes=8 * 1024 * 1024),
    )(*results)


def solution(mesh):
    return jax.shard_map(
        functools.partial(on_device, mesh.shape["seq"], mesh.shape["head"]),
        mesh=mesh,
        in_specs=(
            P("seq", "head"),
            P("seq", "head"),
            P("seq", "head"),
            P("seq", "head"),
            P("head"),
            P("seq", "head"),
        ),
        out_specs=(P("seq", "head"), P("seq", "head"), P("seq", "head"), P("seq", "head")),
        check_vma=False,
    )
```

time: 91.9 us -> 75.7 us (0.82); the launches traced: 90.4 us -> 75.5 us
  Pallas kernels: 83.2 us -> 74.8 us
  local copies, waits for them, and re-layouts: 6.53 us -> 0 us
    pallas_call x1 -> x2, Pallas kernels: 83.2 us -> 74.8 us  [the longest x1 72.8 us: on_device(): pl.pallas_call(functools.partial(kernel, planes, heads, head_count, heads...]
    unnamed x10 -> x0, local copies, waits for them, and re-layouts: 6.53 us -> none
where the time goes in v2:
time: 75.7 us; the launch traced here: 75.5 us
  Pallas kernels  74.8 us (99%)
    pallas_call x1, Pallas kernels, on_device(): pl.pallas_call(functools.partial(kernel, planes, heads, head_count, heads...  72.8 us
    pallas_call x1, Pallas kernels, on_device(): pl.pallas_call(store_kernel, out_shape=(jax.ShapeDtypeStruct((tokens, wid...  2.04 us

profile of v2, /device:TPU:1, one launch (start us, length us, event | category | flops | bytes accessed | tf_op | source)
XLA Modules:
  0.0 75.5 jit_solution(14290688264349947704)
XLA Ops:
  0.6 72.8 %shard_map.93 = (bf16[512,1024]{1,0:T(8,128)(2,1)S(1)}, bf16[512,1024]{1,0:T(8,128)(2,1)S(1)}, bf16[512,1024]{1,0:T(8,128)(2,1)S(1)}, bf16[512,1024]{1,0:T(8,128)(2,1)S(1)}) custom-call(f32[8,512]{1,0:T(8,128)} %bitcast.2, f32[1,1024]{1,0:T(1,128)} %bitcast.3, bf16[512,1024]{1,0:T(8,128)(2,1)} %query_hbm.1, bf16[512,1024]{1,0:T(8,128)(2,1)} %key_hbm.1, ...), custom_call_target="tpu_custom_call" | custom-call | tf_op jit(solution)/shard_map/pallas_call | solution.py:427
  73.4 2.0 %shard_map.94 = (bf16[512,1024]{1,0:T(8,128)(2,1)}, bf16[512,1024]{1,0:T(8,128)(2,1)}, bf16[512,1024]{1,0:T(8,128)(2,1)}, bf16[512,1024]{1,0:T(8,128)(2,1)}) custom-call(bf16[512,1024]{1,0:T(8,128)(2,1)S(1)} %get-tuple-element.8.refs_0_, bf16[512,1024]{1,0:T(8,128)(2,1)S(1)} %get-tuple-element.9.refs_1_, bf16[512,1024]{1,0:T(8,128)(2,1)S(1)} %get-tuple-element.10.refs_2_, ...), custom_call_target="tpu_custom_call" | custom-call | tf_op jit(solution)/shard_map/pallas_call | solution.py:460

commit v3 on v2

--- a/solution.py
+++ b/solution.py
@@ -10,6 +10,7 @@
 DIM = 128
 BLOCK = 512
 HALF = 256
+PARTS = 2
 EPSILON = 1e-06
 F32 = jnp.float32
 BF16 = jnp.bfloat16
@@ -40,12 +41,12 @@
 
 
 def kernel(
-    planes, plane_size, head_count, heads, early, early_back,
-    log_ref, gain_ref, query_hbm, key_hbm, value_hbm, cot_hbm,
+    parts, planes, plane_size, head_count, heads,
+    log_hbm, gain_hbm, query_hbm, key_hbm, value_hbm, cot_hbm,
     att, gq, gk, gv,
-    query, key, value, cot,
+    log_ref, gain_ref, query, key, value, cot,
     cum_row, cum_col, lead, trail, decay0, decay1, weight0, weight1,
-    out, scaled, query_high, query_low, grad, inner_key, inner_value,
+    out, scaled, turned_query, grad, inner_key, inner_value,
     own_total, totals,
     piece, arrived, before, state,
     grad_piece, grad_arrived, after, after_state,
@@ -58,23 +59,14 @@
     place = lax.axis_index("head")
     seq_count = planes * plane_size
     rows = piece.shape[1]
-    half_rows = rows // 2
+    part_size = rows // parts
     features = head_count * heads * DIM
-
-    loads = [
-        pltpu.make_async_copy(source, target, in_sem.at[i])
-        for i, (source, target) in enumerate(
-            ((key_hbm, key), (value_hbm, value), (query_hbm, query), (cot_hbm, cot))
-        )
-    ]
-    for load in loads:
-        load.start()
 
     barrier = pltpu.get_barrier_semaphore()
 
     def greet_seq(d, carry):
         pl.semaphore_signal(
-            barrier, inc=1, device_id={"seq": lax.rem(me + d, seq_count)},
+            barrier, inc=1, device_id={"seq": lax.rem(me + d + seq_count // 2, seq_count)},
             device_id_type=pl.DeviceIdType.MESH,
         )
         return carry
@@ -86,8 +78,20 @@
         )
         return carry
 
-    lax.fori_loop(1, seq_count, greet_seq, 0)
+    lax.fori_loop(0, seq_count // 2, greet_seq, 0)
+    lax.fori_loop(seq_count // 2 + 1, seq_count, greet_seq, 0)
     lax.fori_loop(1, head_count, greet_head, 0)
+    loads = [
+        pltpu.make_async_copy(source, target, in_sem.at[i])
+        for i, (source, target) in enumerate(
+            (
+                (log_hbm, log_ref), (key_hbm, key), (value_hbm, value),
+                (query_hbm, query), (cot_hbm, cot), (gain_hbm, gain_ref),
+            )
+        )
+    ]
+    for load in loads:
+        load.start()
 
     def columns(h):
         return pl.ds(pl.multiple_of(h * DIM, DIM), DIM)
@@ -96,7 +100,7 @@
         return plane_size // 2 + (1 - 2 * lax.rem(i, 2)) * ((i + 1) // 2)
 
     def part_rows(part):
-        return pl.ds(part * half_rows, half_rows)
+        return pl.ds(part * part_size, part_size)
 
     def slots(h):
         return pl.ds(pl.multiple_of(h * planes, planes), planes)
@@ -176,10 +180,13 @@
     lower = lax.broadcasted_iota(jnp.int32, (BLOCK, BLOCK), 0) >= lax.broadcasted_iota(
         jnp.int32, (BLOCK, BLOCK), 1
     )
-    cumulative = lax.dot_general(
-        log_ref[...], lower.astype(F32), NT,
-        precision=lax.Precision.HIGHEST, preferred_element_type=F32,
-    )
+    lower = lower.astype(F32).astype(BF16)
+    loads[0].wait()
+    logs = log_ref[...]
+    high, low = split(logs)
+    rest = (logs - high.astype(F32) - low.astype(F32)).astype(BF16)
+    terms = mul(jnp.concatenate([high, low, rest], axis=0), lower, NT)
+    cumulative = terms[:heads] + (terms[heads : 2 * heads] + terms[2 * heads :])
     cum_row[...] = cumulative
     turned = jnp.transpose(jnp.concatenate([cumulative] * (DIM // heads), axis=0))
     for h in range(heads):
@@ -190,8 +197,8 @@
         for p in range(planes):
             own_total[h * planes + p] = total
 
-    loads[0].wait()
     loads[1].wait()
+    loads[2].wait()
 
     def make_piece(h, carry):
         at = columns(h)
@@ -200,9 +207,18 @@
         store_piece(piece, h, mul(high, both, TN) + mul(low, both, TN))
         return carry
 
-    lax.fori_loop(0, heads, make_piece, 0)
+    def head_at(i):
+        return lax.rem(spot + turn_of(i), plane_size)
+
+    def make_and_give_piece(i, carry):
+        give_head(piece, arrived, 0, 0, head_at(i), False)
+        make_piece(head_at(i + 1), carry)
+        return carry
+
+    make_piece(head_at(0), 0)
     pl.semaphore_wait(barrier, seq_count + head_count - 2)
-    give_all(piece, arrived, 0, 0)
+    lax.fori_loop(0, heads - 1, make_and_give_piece, 0)
+    give_head(piece, arrived, 0, 0, spot, True)
 
     pltpu.make_async_copy(
         own_total.at[spot * planes + plane], totals.at[me], total_sem.at[1]
@@ -215,10 +231,11 @@
         return carry
 
     lax.fori_loop(1, seq_count, share_total, 0)
-    give_all(piece, arrived, 0, 1)
-
-    loads[2].wait()
-    loads[3].wait()
+    for part in range(1, parts):
+        give_all(piece, arrived, 0, part)
+
+    for load in loads[3:]:
+        load.wait()
     causal = lax.broadcasted_iota(jnp.int32, (HALF, HALF), 0) >= lax.broadcasted_iota(
         jnp.int32, (HALF, HALF), 1
     )
@@ -252,30 +269,27 @@
 
         def one(b, running):
             before[b, at] = running
-            return jnp.exp(totals[b]) * running + arrived[b, at]
-
-        lax.fori_loop(0, seq_count, one, jnp.zeros((half_rows, DIM), F32))
+            return totals[b] * running + arrived[b, at]
+
+        lax.fori_loop(0, seq_count, one, jnp.zeros((part_size, DIM), F32), unroll=4)
 
     def prepare(h, carry):
         at = columns(h)
         grown = jnp.exp(cum_col[:, at])
         lead[:, at] = grown
-        high, low = split(query[:, at].astype(F32) * grown)
-        query_high[:, at] = high
-        query_low[:, at] = low
+        high, low = split(jnp.transpose(query[:, at].astype(F32) * grown))
+        turned_query[h] = jnp.concatenate([high, low], axis=0)
         scaled[:, at] = cot[:, at].astype(F32) * gain_ref[:, at]
         return carry
 
-    lax.fori_loop(0, early, forward, 0)
+    lax.fori_loop(0, heads, forward, 0)
+    lax.fori_loop(0, heads, prepare, 0)
     pltpu.make_async_copy(totals, totals, total_sem.at[1]).wait()
-    given(arrived, 0, 0)
-    advance(0)
-    take_all(before, state, 0, 0)
-    lax.fori_loop(early, heads, forward, 0)
-    given(arrived, 0, 1)
-    advance(1)
-    take_all(before, state, 0, 1)
-    lax.fori_loop(0, heads, prepare, 0)
+    totals[...] = jnp.exp(totals[...])
+    for part in range(parts):
+        given(arrived, 0, part)
+        advance(part)
+        take_all(before, state, 0, part)
 
     def finish_out(i, carry):
         squares, inners = carry
@@ -290,11 +304,13 @@
 
     zero = jnp.zeros((BLOCK, DIM), F32)
     squares, inners = lax.fori_loop(0, heads, finish_out, (zero, zero))
-    square_row = jnp.sum(jnp.transpose(squares), axis=0, keepdims=True)
-    inner_row = jnp.sum(jnp.transpose(inners), axis=0, keepdims=True)
-    for i in range(BLOCK // DIM):
-        stat[i : i + 1, :] = square_row[:, i * DIM : (i + 1) * DIM]
-        stat[4 + i : 5 + i, :] = inner_row[:, i * DIM : (i + 1) * DIM]
+    lanes = lax.broadcasted_iota(jnp.int32, (DIM, DIM), 1)
+    packed = jnp.zeros((DIM, DIM), F32)
+    for which, sums in enumerate((squares, inners)):
+        sums = jnp.sum(sums, axis=1, keepdims=True)
+        for i in range(BLOCK // DIM):
+            packed = jnp.where(lanes == 4 * which + i, sums[i * DIM : (i + 1) * DIM], packed)
+    stat[...] = jnp.transpose(packed)[:8]
     pltpu.make_async_copy(stat, stats.at[place], stat_sem.at[1]).start()
 
     def share_stat(d, carry):
@@ -310,13 +326,15 @@
     inverse_rows = lax.rsqrt(summed[:4] / features + EPSILON)
     mean_rows = inverse_rows * summed[4:] / features
 
-    def to_columns(four):
+    turned = jnp.transpose(jnp.concatenate([inverse_rows, mean_rows] * (DIM // 8), axis=0))
+
+    def to_columns(first):
         return jnp.concatenate(
-            [jnp.transpose(jnp.broadcast_to(four[i : i + 1], (DIM, DIM))) for i in range(4)], axis=0
+            [jnp.broadcast_to(turned[:, i : i + 1], (DIM, DIM)) for i in range(first, first + 4)], axis=0
         )
 
-    inverse = to_columns(inverse_rows)
-    mean_term = to_columns(mean_rows)
+    inverse = to_columns(0)
+    mean_term = to_columns(4)
 
     def make_grad(i, carry):
         h = lax.rem(spot + turn_of(i), plane_size)
@@ -325,9 +343,8 @@
         out[:, at] = normed
         g = (inverse * (scaled[:, at] - normed * mean_term)).astype(BF16)
         grad[:, at] = g
-        store_piece(
-            grad_piece, h, mul(query_high[:, at], g, TN) + mul(query_low[:, at], g, TN)
-        )
+        both = mul(turned_query[h], g, NN)
+        store_piece(grad_piece, h, both[:DIM] + both[DIM:])
         return h
 
     def make_and_give(i, carry):
@@ -337,7 +354,8 @@
     lax.fori_loop(0, heads - 1, make_and_give, 0)
     make_grad(heads - 1, 0)
     give_head(grad_piece, grad_arrived, 1, 0, spot, True)
-    give_all(grad_piece, grad_arrived, 1, 1)
+    for part in range(1, parts):
+        give_all(grad_piece, grad_arrived, 1, part)
 
     def backward(h, carry):
         at = columns(h)
@@ -370,19 +388,15 @@
         def one(turn, running):
             b = seq_count - 1 - turn
             after[b, at] = running
-            return grad_arrived[b, at] + jnp.exp(totals[b]) * running
-
-        lax.fori_loop(0, seq_count, one, jnp.zeros((half_rows, DIM), F32))
-
-    lax.fori_loop(0, early_back, backward, 0)
-    given(grad_arrived, 1, 0)
-    retreat(0)
-    take_all(after, after_state, 1, 0)
-    lax.fori_loop(early_back, early_back + 2, backward, 0)
-    given(grad_arrived, 1, 1)
-    retreat(1)
-    take_all(after, after_state, 1, 1)
-    lax.fori_loop(early_back + 2, heads, backward, 0)
+            return grad_arrived[b, at] + totals[b] * running
+
+        lax.fori_loop(0, seq_count, one, jnp.zeros((part_size, DIM), F32), unroll=4)
+
+    lax.fori_loop(0, heads, backward, 0)
+    for part in range(parts):
+        given(grad_arrived, 1, part)
+        retreat(part)
+        take_all(after, after_state, 1, part)
 
     def finish(i, carry):
         h = lax.rem(spot + plane_size - turn_of(i), plane_size)
@@ -406,7 +420,7 @@
     some = stats.at[pl.ds(0, head_count - 1)]
     pltpu.make_async_copy(some, some, stat_sem.at[0]).wait()
     for which in range(2):
-        for part in range(2):
+        for part in range(parts):
             sent(piece, give_send.at[which, part])
             sent(piece, take_send.at[which, part])
 
@@ -423,13 +437,14 @@
     chunk = pltpu.VMEM((seq_count, rows, DIM), F32)
     line = pltpu.VMEM((seq_count, 1, DIM), F32)
     pair = pltpu.SemaphoreType.DMA((2,))
-    square = pltpu.SemaphoreType.DMA((2, 2))
+    square = pltpu.SemaphoreType.DMA((2, PARTS))
     results = pl.pallas_call(
-        functools.partial(kernel, planes, heads, head_count, heads, 4, 3),
+        functools.partial(kernel, PARTS, planes, heads, head_count, heads),
         out_shape=(narrow,) * 4,
-        in_specs=[vmem, vmem] + [hbm] * 4,
+        in_specs=[hbm] * 6,
         out_specs=(vmem,) * 4,
-        scratch_shapes=[narrow] * 4
+        scratch_shapes=[pltpu.VMEM((heads, tokens), F32), pltpu.VMEM((1, width), F32)]
+        + [narrow] * 4
         + [
             pltpu.VMEM((heads, tokens), F32),
             wide,
@@ -441,8 +456,7 @@
             pltpu.VMEM((heads, HALF, BLOCK), BF16),
             wide,
             wide,
-            narrow,
-            narrow,
+            pltpu.VMEM((heads, 2 * DIM, tokens), BF16),
             narrow,
             wide,
             wide,
@@ -451,7 +465,7 @@
         ]
         + [chunk] * 8
         + [pltpu.VMEM((8, DIM), F32), pltpu.VMEM((head_count, 8, DIM), F32)]
-        + [pltpu.SemaphoreType.DMA((4,)), pair, pair, square, square, square]
+        + [pltpu.SemaphoreType.DMA((6,)), pair, pair, square, square, square]
         + [pltpu.SemaphoreType.DMA((2, heads))],
         compiler_params=pltpu.CompilerParams(
             collective_id=0, has_side_effects=True, vmem_limit_bytes=59 * 1024 * 1024

time: 75.7 us -> 75.1 us (level)
  no operation moved by 1% of the time
where the time goes in v3:
time: 75.1 us; the launch traced here: 75 us
  Pallas kernels  74.3 us (99%)
    pallas_call x1, Pallas kernels, on_device(): pl.pallas_call(functools.partial(kernel, PARTS, planes, heads, head_count...  72.3 us
    pallas_call x1, Pallas kernels, on_device(): pl.pallas_call(store_kernel, out_shape=(jax.ShapeDtypeStruct((tokens, wid...  2.04 us

profile of v3, /device:TPU:1, one launch (start us, length us, event | category | flops | bytes accessed | tf_op | source)
XLA Modules:
  0.0 75.0 jit_solution(11406086256187509066)
XLA Ops:
  0.6 72.3 %shard_map.93 = (bf16[512,1024]{1,0:T(8,128)(2,1)S(1)}, bf16[512,1024]{1,0:T(8,128)(2,1)S(1)}, bf16[512,1024]{1,0:T(8,128)(2,1)S(1)}, bf16[512,1024]{1,0:T(8,128)(2,1)S(1)}) custom-call(f32[8,512]{1,0:T(8,128)} %bitcast.2, f32[1,1024]{1,0:T(1,128)} %bitcast.3, bf16[512,1024]{1,0:T(8,128)(2,1)} %query_hbm.1, bf16[512,1024]{1,0:T(8,128)(2,1)} %key_hbm.1, ...), custom_call_target="tpu_custom_call" | custom-call | tf_op jit(solution)/shard_map/pallas_call | solution.py:441
  72.9 2.0 %shard_map.94 = (bf16[512,1024]{1,0:T(8,128)(2,1)}, bf16[512,1024]{1,0:T(8,128)(2,1)}, bf16[512,1024]{1,0:T(8,128)(2,1)}, bf16[512,1024]{1,0:T(8,128)(2,1)}) custom-call(bf16[512,1024]{1,0:T(8,128)(2,1)S(1)} %get-tuple-element.8.refs_0_, bf16[512,1024]{1,0:T(8,128)(2,1)S(1)} %get-tuple-element.9.refs_1_, bf16[512,1024]{1,0:T(8,128)(2,1)S(1)} %get-tuple-element.10.refs_2_, ...), custom_call_target="tpu_custom_call" | custom-call | tf_op jit(solution)/shard_map/pallas_call | solution.py:474

commit v4 on v3

--- a/solution.py
+++ b/solution.py
@@ -97,7 +97,7 @@
         return pl.ds(pl.multiple_of(h * DIM, DIM), DIM)
 
     def turn_of(i):
-        return plane_size // 2 + (1 - 2 * lax.rem(i, 2)) * ((i + 1) // 2)
+        return lax.rem(plane_size // 2 + (1 - 2 * lax.rem(place, 2)) * (1 - 2 * lax.rem(i, 2)) * ((i + 1) // 2), plane_size)
 
     def part_rows(part):
         return pl.ds(part * part_size, part_size)
@@ -113,8 +113,8 @@
 
     def give_head(source, target, which, part, h, own):
         at = part_rows(part)
-        for d in range(planes):
-            p = lax.rem(plane + d, planes)
+        for d in (2, 1, 3, 0):
+            p = lax.rem(plane + d * (1 + 2 * lax.rem(place, 2)), planes)
             if own and d == 0:
                 pltpu.make_async_copy(
                     source.at[h * planes + p, at], target.at[me, at], give_receive.at[which, part]
@@ -139,8 +139,8 @@
         slot = spot * planes + plane
 
         def one_spot(z, own):
-            for d in range(planes):
-                p = lax.rem(plane + d, planes)
+            for d in (2, 1, 3, 0):
+                p = lax.rem(plane + d * (1 + 2 * lax.rem(place, 2)), planes)
                 b = p * plane_size + z
                 if own and d == 0:
                     pltpu.make_async_copy(

time: 75.1 us -> 74.4 us (level)
  no operation moved by 1% of the time
where the time goes in v4:
time: 74.4 us; the launch traced here: 74.3 us
  Pallas kernels  73.6 us (99%)
    pallas_call x1, Pallas kernels, on_device(): pl.pallas_call(functools.partial(kernel, PARTS, planes, heads, head_count...  71.6 us
    pallas_call x1, Pallas kernels, on_device(): pl.pallas_call(store_kernel, out_shape=(jax.ShapeDtypeStruct((tokens, wid...  2.04 us

profile of v4, /device:TPU:1, one launch (start us, length us, event | category | flops | bytes accessed | tf_op | source)
XLA Modules:
  0.0 74.3 jit_solution(13068310016556059028)
XLA Ops:
  0.6 71.6 %shard_map.93 = (bf16[512,1024]{1,0:T(8,128)(2,1)S(1)}, bf16[512,1024]{1,0:T(8,128)(2,1)S(1)}, bf16[512,1024]{1,0:T(8,128)(2,1)S(1)}, bf16[512,1024]{1,0:T(8,128)(2,1)S(1)}) custom-call(f32[8,512]{1,0:T(8,128)} %bitcast.2, f32[1,1024]{1,0:T(1,128)} %bitcast.3, bf16[512,1024]{1,0:T(8,128)(2,1)} %query_hbm.1, bf16[512,1024]{1,0:T(8,128)(2,1)} %key_hbm.1, ...), custom_call_target="tpu_custom_call" | custom-call | tf_op jit(solution)/shard_map/pallas_call | solution.py:441
  72.2 2.0 %shard_map.94 = (bf16[512,1024]{1,0:T(8,128)(2,1)}, bf16[512,1024]{1,0:T(8,128)(2,1)}, bf16[512,1024]{1,0:T(8,128)(2,1)}, bf16[512,1024]{1,0:T(8,128)(2,1)}) custom-call(bf16[512,1024]{1,0:T(8,128)(2,1)S(1)} %get-tuple-element.8.refs_0_, bf16[512,1024]{1,0:T(8,128)(2,1)S(1)} %get-tuple-element.9.refs_1_, bf16[512,1024]{1,0:T(8,128)(2,1)S(1)} %get-tuple-element.10.refs_2_, ...), custom_call_target="tpu_custom_call" | custom-call | tf_op jit(solution)/shard_map/pallas_call | solution.py:474

commit v5 on v4

--- a/solution.py
+++ b/solution.py
@@ -131,7 +131,7 @@
             give_head(source, target, which, part, lax.rem(spot + turn_of(i), plane_size), False)
             return carry
 
-        lax.fori_loop(0, plane_size - 1, one, 0)
+        lax.fori_loop(0, plane_size - 1, one, 0, unroll=True)
         give_head(source, target, which, part, spot, True)
 
     def take_all(source, target, which, part):
@@ -156,7 +156,7 @@
             one_spot(lax.rem(spot + turn_of(i), plane_size), False)
             return carry
 
-        lax.fori_loop(0, plane_size - 1, one, 0)
+        lax.fori_loop(0, plane_size - 1, one, 0, unroll=True)
         one_spot(spot, True)
 
     def given(target, which, part):
@@ -271,7 +271,7 @@
             before[b, at] = running
             return totals[b] * running + arrived[b, at]
 
-        lax.fori_loop(0, seq_count, one, jnp.zeros((part_size, DIM), F32), unroll=4)
+        lax.fori_loop(0, seq_count, one, jnp.zeros((part_size, DIM), F32), unroll=8)
 
     def prepare(h, carry):
         at = columns(h)
@@ -313,12 +313,13 @@
     stat[...] = jnp.transpose(packed)[:8]
     pltpu.make_async_copy(stat, stats.at[place], stat_sem.at[1]).start()
 
-    def share_stat(d, carry):
+    def share_stat(i, carry):
+        d = head_count // 2 + (1 - 2 * lax.rem(i, 2)) * ((i + 1) // 2)
         peer = lax.rem(place + d, head_count)
         remote(stat, stats.at[place], stat_sem.at[0], stat_sem.at[1], {"head": peer})
         return carry
 
-    lax.fori_loop(1, head_count, share_stat, 0)
+    lax.fori_loop(0, head_count - 1, share_stat, 0, unroll=True)
     pltpu.make_async_copy(stats, stats, stat_sem.at[1]).wait()
     summed = stats[0]
     for i in range(1, head_count):
@@ -390,7 +391,7 @@
             after[b, at] = running
             return grad_arrived[b, at] + totals[b] * running
 
-        lax.fori_loop(0, seq_count, one, jnp.zeros((part_size, DIM), F32), unroll=4)
+        lax.fori_loop(0, seq_count, one, jnp.zeros((part_size, DIM), F32), unroll=8)
 
     lax.fori_loop(0, heads, backward, 0)
     for part in range(parts):

time: 74.4 us -> 74.4 us (level)
  no operation moved by 1% of the time
where the time goes in v5:
time: 74.4 us; the launch traced here: 74.2 us
  Pallas kernels  73.6 us (99%)
    pallas_call x1, Pallas kernels, on_device(): pl.pallas_call(functools.partial(kernel, PARTS, planes, heads, head_count...  71.5 us
    pallas_call x1, Pallas kernels, on_device(): pl.pallas_call(store_kernel, out_shape=(jax.ShapeDtypeStruct((tokens, wid...  2.04 us

profile of v5, /device:TPU:1, one launch (start us, length us, event | category | flops | bytes accessed | tf_op | source)
XLA Modules:
  0.0 74.2 jit_solution(11894056360585302321)
XLA Ops:
  0.6 71.5 %shard_map.93 = (bf16[512,1024]{1,0:T(8,128)(2,1)S(1)}, bf16[512,1024]{1,0:T(8,128)(2,1)S(1)}, bf16[512,1024]{1,0:T(8,128)(2,1)S(1)}, bf16[512,1024]{1,0:T(8,128)(2,1)S(1)}) custom-call(f32[8,512]{1,0:T(8,128)} %bitcast.2, f32[1,1024]{1,0:T(1,128)} %bitcast.3, bf16[512,1024]{1,0:T(8,128)(2,1)} %query_hbm.1, bf16[512,1024]{1,0:T(8,128)(2,1)} %key_hbm.1, ...), custom_call_target="tpu_custom_call" | custom-call | tf_op jit(solution)/shard_map/pallas_call | solution.py:442
  72.2 2.0 %shard_map.94 = (bf16[512,1024]{1,0:T(8,128)(2,1)}, bf16[512,1024]{1,0:T(8,128)(2,1)}, bf16[512,1024]{1,0:T(8,128)(2,1)}, bf16[512,1024]{1,0:T(8,128)(2,1)}) custom-call(bf16[512,1024]{1,0:T(8,128)(2,1)S(1)} %get-tuple-element.8.refs_0_, bf16[512,1024]{1,0:T(8,128)(2,1)S(1)} %get-tuple-element.9.refs_1_, bf16[512,1024]{1,0:T(8,128)(2,1)S(1)} %get-tuple-element.10.refs_2_, ...), custom_call_target="tpu_custom_call" | custom-call | tf_op jit(solution)/shard_map/pallas_call | solution.py:475
